TPU v7x, 32 devices: a whole 2x2x4 slice. The times are simulated.
32 devices in a mesh: tm: 8 (over y, x, core), group: 4 (over z).
Axes of the slice: x: 2, y: 2, z: 4, core: 2. Of those that a mesh axis runs over, the one named last changes fastest.
Arguments:
- propagators: float32 [8, 384, 384], P('tm'), may hold values from -1 to 1, as said below
- perturbation: float32 [8, 384, 384], P('tm', 'group'), as said below
Outputs:
- gradient: float32 [384, 384], P('tm')
Inputs may be any that keep to these rules, and one draw needn't show every extreme that they name: `propagators`: each slice's matrix is orthogonal. `perturbation`: each slice's matrix is symmetric.
All inputs are finite; a program needn't handle non-finite values.
Results may differ from a plain program's by a relative error of at most 0.00028.
Values sent between devices are 32-bit elements; how exact they have to be, the bound alone decides.
No kernel may reach another device: no remote copies, remote signals or barrier semaphores. Data moves between devices by JAX's collectives and lax.ppermute only.
A program may use at most 128 MiB of HBM per device.

v0:
```python
import jax
import jax.numpy as jnp
from jax import lax
from jax.sharding import PartitionSpec as P


def carried_in(part, axis, combine, identity):
    place = lax.axis_index(axis)
    gathered = lax.all_gather(part, axis)
    state = jnp.zeros_like(part) + jnp.asarray(identity, part.dtype)

    def one(lap, state):
        return combine(state, lax.dynamic_index_in_dim(gathered, lap, 0, False))

    return lax.fori_loop(0, place, one, state)


def times_high(left, right):
    return jnp.dot(left, right, precision=lax.Precision.HIGHEST, preferred_element_type=jnp.float32)


def compose(earlier, later):
    return times_high(later, earlier)


def body(propagators, perturbation):
    slice_count = propagators.shape[0]
    order_dim = propagators.shape[1]
    block_rows = perturbation.shape[1]
    identity = jnp.eye(order_dim, dtype=jnp.float32)
    local_prefixes = [identity]
    device_total = times_high(propagators[slice_count - 1], local_prefixes[-1])
    before = carried_in(device_total, "tm", compose, identity)
    first_block = lax.axis_index("group") * block_rows
    prefix_rows = lax.dynamic_slice_in_dim(before, first_block, block_rows, 0)
    pulled = times_high(perturbation[0], before)
    conjugated = times_high(prefix_rows.T, pulled)
    row_sums = lax.psum_scatter(conjugated, "tm", scatter_dimension=0, tiled=True)
    return lax.psum(row_sums, "group")


def solution(mesh):
    in_specs = (P("tm", None, None), P("tm", "group", None))
    out_specs = P("tm", None)
    return jax.shard_map(body, mesh=mesh, in_specs=in_specs, out_specs=out_specs, check_vma=False)
```

profile of v0, /device:TPU:0, one launch (start us, length us, event | category | flops | bytes accessed | tf_op | source)
XLA Modules:
  0.0 155.6 jit_solution(5823865246684013293)
XLA Ops:
  6.5 0.0 copy-start
  6.5 0.0 all-gather.3.cloned.1.call-start
  6.5 1.1 copy-done
  7.6 1.6 %convolution_bitcast_fusion = f32[384,384]{0,1:T(8,128)} fusion(f32[1,384,384]{2,1,0:T(8,128)S(1)} %copy-done), kind=kOutput, calls=%fused_computation.4 | convolution fusion | flops 679772160 | bytes 1179648 | tf_op jit(solution)/shard_map/dot_general | solution.py:19
  9.2 0.0 all-gather.3.cloned.1.call-update
  9.2 0.0 reduce-scatter.2.cloned.1.call-start
  9.3 41.5 %all-gather.3.cloned.1.call-done = f32[3072,384]{0,1:T(8,128)} async-done(((f32[384,384]{0,1:T(8,128)}), f32[3072,384]{0,1:T(8,128)}) %all-gather.3.cloned.1.call-update) | async-done | bytes 4718608 | tf_op jit(solution)/shard_map/all_gather | solution.py:9
  50.8 6.1 %copy.4 = f32[3072,384]{1,0:T(8,128)} copy(f32[3072,384]{0,1:T(8,128)} %all-gather.3.cloned.1.call-done) | data formatting | bytes 9437184 | tf_op jit(solution)/shard_map/while | solution.py:15
  56.9 0.0 copy-start.1
  56.9 0.9 copy-done.1
  57.8 1.1 fusion.8
  58.9 1.7 %fusion.10 = f32[384,384]{1,0:T(8,128)} fusion(f32[384,96]{1,0:T(8,128)S(1)} %fusion.8, f32[384,384]{1,0:T(8,128)S(1)} %get-tuple-element.28, s32[]{:T(128)S(6)} %select_n.7), kind=kOutput, calls=%fused_computation.11 | convolution fusion | flops 169869312 | bytes 933892 | tf_op jit(solution)/shard_map/dot_general | solution.py:19
  60.6 0.0 reduce-scatter.2.cloned.1.call-update
  60.6 0.0 all-reduce.2.cloned.1.call-start
  60.7 50.3 %reduce-scatter.2.cloned.1.call-done = f32[48,384]{1,0:T(8,128)} async-done(((f32[384,384]{1,0:T(8,128)}), f32[48,384]{1,0:T(8,128)}) %reduce-scatter.2.cloned.1.call-update) | async-done | bytes 73744 | tf_op jit(solution)/shard_map/reduce_scatter | solution.py:38
  111.0 0.0 all-reduce.2.cloned.1.call-update
  111.0 36.6 %all-reduce.2.cloned.1.call-done = f32[48,384]{1,0:T(8,128)} async-done(((f32[48,384]{1,0:T(8,128)}), f32[48,384]{1,0:T(8,128)}) %all-reduce.2.cloned.1.call-update) | async-done | bytes 73744 | tf_op jit(solution)/shard_map/psum | solution.py:39
  147.6 1.5 copy.14
  (2 shorter events, 0.0 us)
Async XLA Ops:
  6.5 1.1 copy-start
  6.5 44.3 %all-gather.3.cloned.1.call-start = ((), (), s32[]{:S(2)}) async-start(), calls=%async_computation.3 | async-start | bytes 5308416 | tf_op jit(solution)/shard_map/all_gather | solution.py:9
  9.2 101.7 %reduce-scatter.2.cloned.1.call-start = ((), (), s32[]{:S(2)}) async-start(), calls=%async_computation.1 | async-start | bytes 663552 | tf_op jit(solution)/shard_map/reduce_scatter | solution.py:38
  56.9 0.9 copy-start.1
  60.6 86.9 %all-reduce.2.cloned.1.call-start = ((), (), s32[]{:S(2)}) async-start(), calls=%async_computation.2 | async-start | bytes 147456 | tf_op jit(solution)/shard_map/psum | solution.py:39
Sparse Core Ops, SparseCore 0:
  9.4 41.4 all-gather.2
  60.7 50.1 reduce-scatter.1
  113.3 34.2 all-reduce.1
where the time goes:
time: 156 us
  waiting for transfers between devices  128 us (82%)
  between operations  13.1 us (8%)
  local copies, waits for them, and re-layouts  9.54 us (6%)
  matrix products  4.43 us (3%)
    reduce_scatter x1, waiting for transfers between devices, body(): lax.psum_scatter(conjugated, 'tm', scatter_dimension=0, tiled=True)  50.3 us
    all_gather x1, waiting for transfers between devices, carried_in(): gathered = lax.all_gather(part, axis)  41.5 us
    psum x1, waiting for transfers between devices, body(): return lax.psum(row_sums, 'group')  36.6 us
    while x1, local copies, waits for them, and re-layouts, carried_in(): return lax.fori_loop(0, place, one, state)  6.05 us
    dot_general x3, matrix products, times_high(): jnp.dot(left, right, precision=lax.Precision.HIGHEST, preferred_element_t...  4.43 us
    unnamed x5, local copies, waits for them, and re-layouts  3.49 us
  transfers between devices with their start and end apart: 3, of which 3 were waited for; matrix products, arithmetic and copies ran while one was open for 0% of the time, Pallas kernels for 0%

commit v1 on v0

--- a/solution.py
+++ b/solution.py
@@ -2,6 +2,7 @@
 import jax.numpy as jnp
 from jax import lax
 from jax.sharding import PartitionSpec as P
+from jax.lax import all_gather
 
 
 def carried_in(part, axis, combine, identity):
@@ -36,7 +37,7 @@
     pulled = times_high(perturbation[0], before)
     conjugated = times_high(prefix_rows.T, pulled)
     row_sums = lax.psum_scatter(conjugated, "tm", scatter_dimension=0, tiled=True)
-    return lax.psum(row_sums, "group")
+    return all_gather(row_sums, "group").sum(axis=0)
 
 
 def solution(mesh):

time: 156 us -> 133 us (0.85)
  waiting for transfers between devices: 128 us -> 91.8 us
  blocking collectives: 0 us -> 14.3 us
    psum x1 -> x0, waiting for transfers between devices: 36.6 us -> none  [body(): return lax.psum(row_sums, 'group')]
    all_gather x0 -> x1, blocking collectives: none -> 14.3 us  [body(): return all_gather(row_sums, 'group').sum(axis=0)]
    unnamed x5 -> x4, local copies, waits for them, and re-layouts: 3.49 us -> 1.97 us
  transfers between devices with their start and end apart: 3 -> 2, of which waited for: 3 -> 2; matrix products, arithmetic and copies ran while one was open for 0% -> 0% of each run, Pallas kernels for 0% -> 0%
where the time goes in v1:
time: 133 us
  waiting for transfers between devices  91.8 us (69%)
  blocking collectives  14.3 us (11%)
  between operations  13.4 us (10%)
  local copies, waits for them, and re-layouts  8.02 us (6%)
  matrix products  4.42 us (3%)
    reduce_scatter x1, waiting for transfers between devices, body(): lax.psum_scatter(conjugated, 'tm', scatter_dimension=0, tiled=True)  50.3 us
    all_gather x1, waiting for transfers between devices, carried_in(): gathered = lax.all_gather(part, axis)  41.5 us
    all_gather x1, blocking collectives, body(): return all_gather(row_sums, 'group').sum(axis=0)  14.3 us
    while x1, local copies, waits for them, and re-layouts, carried_in(): return lax.fori_loop(0, place, one, state)  6.05 us
    dot_general x3, matrix products, times_high(): jnp.dot(left, right, precision=lax.Precision.HIGHEST, preferred_element_t...  4.42 us
  transfers between devices with their start and end apart: 2, of which 2 were waited for; matrix products, arithmetic and copies ran while one was open for 0% of the time, Pallas kernels for 0%

profile of v1, /device:TPU:0, one launch (start us, length us, event | category | flops | bytes accessed | tf_op | source)
XLA Modules:
  0.0 132.8 jit_solution(10868188667320480218)
XLA Ops:
  6.5 0.0 copy-start
  6.5 0.0 all-gather.4.cloned.1.call-start
  6.5 1.1 copy-done
  7.6 1.6 %convolution_bitcast_fusion = f32[384,384]{0,1:T(8,128)} fusion(f32[1,384,384]{2,1,0:T(8,128)S(1)} %copy-done), kind=kOutput, calls=%fused_computation.4 | convolution fusion | flops 679772160 | bytes 1179648 | tf_op jit(solution)/shard_map/dot_general | solution.py:20
  9.2 0.0 all-gather.4.cloned.1.call-update
  9.2 0.0 reduce-scatter.2.cloned.1.call-start
  9.3 41.5 %all-gather.4.cloned.1.call-done = f32[3072,384]{0,1:T(8,128)} async-done(((f32[384,384]{0,1:T(8,128)}), f32[3072,384]{0,1:T(8,128)}) %all-gather.4.cloned.1.call-update) | async-done | bytes 4718608 | tf_op jit(solution)/shard_map/all_gather | solution.py:10
  50.8 6.0 %copy.4 = f32[3072,384]{1,0:T(8,128)} copy(f32[3072,384]{0,1:T(8,128)} %all-gather.4.cloned.1.call-done) | data formatting | bytes 9437184 | tf_op jit(solution)/shard_map/while | solution.py:16
  56.9 0.0 copy-start.1
  56.9 0.9 copy-done.1
  57.8 1.1 fusion.8
  58.9 1.7 %fusion.10 = f32[384,384]{1,0:T(8,128)} fusion(f32[384,96]{1,0:T(8,128)S(1)} %fusion.8, f32[384,384]{1,0:T(8,128)S(1)} %get-tuple-element.28, s32[]{:T(128)S(6)} %select_n.7), kind=kOutput, calls=%fused_computation.11 | convolution fusion | flops 169869312 | bytes 933892 | tf_op jit(solution)/shard_map/dot_general | solution.py:20
  60.6 0.0 reduce-scatter.2.cloned.1.call-update
  60.6 50.3 %reduce-scatter.2.cloned.1.call-done = f32[48,384]{1,0:T(8,128)} async-done(((f32[384,384]{1,0:T(8,128)}), f32[48,384]{1,0:T(8,128)}) %reduce-scatter.2.cloned.1.call-update) | async-done | bytes 73744 | tf_op jit(solution)/shard_map/reduce_scatter | solution.py:39
  111.0 14.3 %all-gather.1 = f32[192,384]{1,0:T(8,128)S(1)} all-gather(f32[48,384]{1,0:T(8,128)} %reduce-scatter.2.cloned.1.call-done), channel_id=3, replica_groups=mesh['tm'=8,'group'=4] {'group'}, dimensions={0}, use_global_device_ids=true | all-gather | bytes 368640 | tf_op jit(solution)/shard_map/all_gather | solution.py:40
  125.3 0.7 reduce_sum.9
  (2 shorter events, 0.0 us)
Async XLA Ops:
  6.5 1.1 copy-start
  6.5 44.3 %all-gather.4.cloned.1.call-start = ((), (), s32[]{:S(2)}) async-start(), calls=%async_computation.2 | async-start | bytes 5308416 | tf_op jit(solution)/shard_map/all_gather | solution.py:10
  9.2 101.7 %reduce-scatter.2.cloned.1.call-start = ((), (), s32[]{:S(2)}) async-start(), calls=%async_computation.1 | async-start | bytes 663552 | tf_op jit(solution)/shard_map/reduce_scatter | solution.py:39
  56.9 0.9 copy-start.1
Sparse Core Ops, SparseCore 0:
  9.4 41.4 all-gather.3
  60.7 50.1 reduce-scatter.1
